TPU v7x, 256 devices: a whole 4x4x8 slice. The times are simulated.
256 devices in a mesh: segment: 4 (over y), mp: 16 (over z, core), dp: 4 (over x).
Axes of the slice: x: 4, y: 4, z: 8, core: 2. Of those that a mesh axis runs over, the one named last changes fastest.
Arguments:
- text_rows: bfloat16 [4, 512, 1024], P(None, 'dp'), may hold values from -6 to 6
- durations: int32 [4, 4, 128], P(None, 'dp'), may hold values from 1 to 16, 512 in all within a row
- unit_targets: int32 [4, 2048], P(None, 'dp'), may hold values from 0 to 9999
- w_in: bfloat16 [4, 1024, 8192], P('segment', None, 'mp'), may hold values from -0.1875 to 0.1875
- w_out: bfloat16 [4, 8192, 1024], P('segment', 'mp'), may hold values from -0.0625 to 0.0625
- w_unit: bfloat16 [1024, 10240], P(None, ('segment', 'mp')), as said below
Outputs:
- loss: float32 [4], P('dp')
- grad_in: float32 [4, 1024, 8192], P('segment', 'dp', 'mp')
- grad_out: float32 [4, 8192, 1024], P('segment', 'mp', 'dp')
- grad_unit: float32 [1024, 10240], P('dp', ('segment', 'mp'))
Inputs may be any that keep to these rules, and one draw needn't show every extreme that they name: Within each micro-batch and each index of dp the 128 durations sum to exactly 512, and one of them equals 16. `w_unit`: entries of order 3 / sqrt(1024) in most columns, some columns much larger.
All inputs are finite; a program needn't handle non-finite values.
Results may differ from a plain program's by a relative error of at most 0.035.
Values may be sent and summed in bfloat16 or wider, within the bound.
A program may use at most 128 MiB of HBM per device.

v0:
```python
import jax
import jax.numpy as jnp
from jax import lax
from jax.sharding import PartitionSpec as P


def shifted(block, axis, distance):
    devices = range(lax.axis_size(axis))
    route = [(i - distance, i) for i in devices if i - distance in devices]
    return lax.ppermute(block, axis, route)


def broadcast(x, axis, root):
    mine = lax.axis_index(axis) == root
    return lax.psum(jnp.where(mine, x, jnp.zeros_like(x)), axis)


def gelu_parts(pre_vals):
    coeff = 0.7978845608
    inner = coeff * (pre_vals + 0.044715 * pre_vals * pre_vals * pre_vals)
    tanh_val = jnp.tanh(inner)
    value = 0.5 * pre_vals * (1.0 + tanh_val)
    slope = 0.5 * (1.0 + tanh_val) + 0.5 * pre_vals * (1.0 - tanh_val * tanh_val) * coeff * (
        1.0 + 3.0 * 0.044715 * pre_vals * pre_vals
    )
    return (value, slope)


def row_scale(rows_in):
    floats = rows_in.astype(jnp.float32)
    return lax.rsqrt(jnp.mean(floats * floats, axis=-1, keepdims=True) + 1e-06)


def norm_back(rows_in, grads):
    scale = row_scale(rows_in)
    normal = rows_in.astype(jnp.float32) * scale
    return scale * (grads - normal * jnp.mean(grads * normal, axis=-1, keepdims=True))


def section(rows_in, first):
    normed = (rows_in.astype(jnp.float32) * row_scale(rows_in)).astype(jnp.bfloat16)
    pre_vals = jnp.dot(normed, first, preferred_element_type=jnp.float32)
    value, slope = gelu_parts(pre_vals)
    return (normed, value.astype(jnp.bfloat16), slope)


def finish_forward(pieces, summed):
    return (pieces[0].astype(jnp.float32) + summed).astype(jnp.bfloat16)


def finish_backward(pieces, summed):
    return (pieces[0].astype(jnp.float32) + norm_back(pieces[1], summed)).astype(jnp.bfloat16)


def reduce_rows(partial_value, pieces, finisher):
    summed = lax.psum(partial_value, "mp")
    return finisher(pieces, summed)


def on_device(text_rows, durations, unit_targets, w_in, w_out, w_unit):
    micro_count, row_count, width = text_rows.shape
    segments = lax.axis_size("segment")
    segment_at = lax.axis_index("segment")
    first = w_in[0]
    second = w_out[0]
    clocks = micro_count + segments - 1
    stash = jnp.zeros((micro_count, row_count, width), jnp.bfloat16)
    final_rows = jnp.zeros((micro_count, row_count, width), jnp.bfloat16)
    outgoing = jnp.zeros((row_count, width), jnp.bfloat16)
    for clock in range(clocks):
        if clock > 0:
            incoming = shifted(outgoing, "segment", 1)
        else:
            incoming = jnp.zeros((row_count, width), jnp.bfloat16)
        rows_in = jnp.where(segment_at == 0, text_rows[min(clock, micro_count - 1)], incoming)
        batch_at = clock - segment_at
        is_live = (batch_at >= 0) & (batch_at < micro_count)
        slot_at = jnp.clip(batch_at, 0, micro_count - 1)
        stash = jnp.where(
            is_live, lax.dynamic_update_index_in_dim(stash, rows_in, slot_at, 0), stash
        )
        normed, hidden, slope = section(rows_in, first)
        partial_value = jnp.dot(hidden, second, preferred_element_type=jnp.float32)
        outgoing = reduce_rows(partial_value, (rows_in,), finish_forward)
        is_last = is_live & (segment_at == segments - 1)
        final_rows = jnp.where(
            is_last, lax.dynamic_update_index_in_dim(final_rows, outgoing, slot_at, 0), final_rows
        )
    final_rows = broadcast(final_rows, "segment", segments - 1)
    vocab_part = w_unit.shape[1]
    vocab_start = lax.axis_index(("segment", "mp")) * vocab_part
    final_norm = (final_rows.astype(jnp.float32) * row_scale(final_rows)).astype(jnp.bfloat16)
    logits = jnp.einsum("mrd,dv->mrv", final_norm, w_unit, preferred_element_type=jnp.float32)
    lengths = durations[:, 0, :]
    unit_count = unit_targets.shape[1]
    ends = jnp.cumsum(lengths, axis=-1)
    positions = jnp.arange(unit_count, dtype=jnp.int32)
    row_local = jnp.sum((ends[:, None, :] <= positions[None, :, None]).astype(jnp.int32), axis=-1)
    row_onehot = (
        row_local[:, :, None] == jnp.arange(row_count, dtype=jnp.int32)[None, None, :]
    ).astype(jnp.bfloat16)
    vocab_ids = vocab_start + jnp.arange(vocab_part, dtype=jnp.int32)
    target_hits = (unit_targets[:, :, None] == vocab_ids[None, None, :]).astype(jnp.bfloat16)
    counts = jnp.einsum("mur,muv->mrv", row_onehot, target_hits, preferred_element_type=jnp.float32)
    local_peak = jnp.max(logits, axis=-1)
    target_local = jnp.sum(counts * logits, axis=-1)
    peak = lax.pmax(local_peak, ("segment", "mp"))
    total, target_sum = lax.psum(
        (jnp.sum(jnp.exp(logits - peak[..., None]), axis=-1), target_local), ("segment", "mp")
    )
    lse = peak + jnp.log(total)
    denom = float(micro_count * unit_count * lax.axis_size("dp"))
    length_f = lengths.astype(jnp.float32)
    loss_local = jnp.sum(length_f * lse - target_sum)
    loss = (loss_local / denom)[None]
    dlogits = ((length_f[..., None] * jnp.exp(logits - lse[..., None]) - counts) / denom).astype(
        jnp.bfloat16
    )
    grad_unit = jnp.einsum("mrd,mrv->dv", final_norm, dlogits, preferred_element_type=jnp.float32)
    norm_part = jnp.einsum("mrv,dv->mrd", dlogits, w_unit, preferred_element_type=jnp.float32)
    norm_share = lax.psum_scatter(
        norm_part, ("segment", "mp"), scatter_dimension=2, tiled=True
    ).astype(jnp.bfloat16)
    dnorm = lax.all_gather(norm_share, ("segment", "mp"), axis=2, tiled=True)
    grad_final = norm_back(final_rows, dnorm.astype(jnp.float32)).astype(jnp.bfloat16)
    grad_first = jnp.zeros(first.shape, jnp.float32)
    grad_second = jnp.zeros(second.shape, jnp.float32)
    going_back = jnp.zeros((row_count, width), jnp.bfloat16)
    for clock in range(clocks):
        if clock > 0:
            arriving = shifted(going_back, "segment", -1)
        else:
            arriving = jnp.zeros((row_count, width), jnp.bfloat16)
        grad_rows = jnp.where(
            segment_at == segments - 1, grad_final[min(clock, micro_count - 1)], arriving
        )
        batch_at = clock - (segments - 1 - segment_at)
        is_live = (batch_at >= 0) & (batch_at < micro_count)
        slot_at = jnp.clip(batch_at, 0, micro_count - 1)
        rows_in = lax.dynamic_index_in_dim(stash, slot_at, 0, keepdims=False)
        normed, hidden, slope = section(rows_in, first)
        live_f = is_live.astype(jnp.float32)
        grad_second = grad_second + live_f * jnp.dot(
            hidden.T, grad_rows, preferred_element_type=jnp.float32
        )
        dhidden = jnp.dot(grad_rows, second.T, preferred_element_type=jnp.float32)
        dpre = (dhidden * slope).astype(jnp.bfloat16)
        grad_first = grad_first + live_f * jnp.dot(
            normed.T, dpre, preferred_element_type=jnp.float32
        )
        dnormed = jnp.dot(dpre, first.T, preferred_element_type=jnp.float32)
        going_back = reduce_rows(dnormed, (grad_rows, rows_in), finish_backward)
    sum_first, sum_second, sum_unit = (
        lax.psum_scatter(grad_first, "dp", scatter_dimension=0, tiled=True),
        lax.psum_scatter(grad_second, "dp", scatter_dimension=1, tiled=True),
        lax.psum_scatter(grad_unit, "dp", scatter_dimension=0, tiled=True),
    )
    return (loss, sum_first[None], sum_second[None], sum_unit)


def solution(mesh):
    placed = (
        P(None, "dp", None),
        P(None, "dp", None),
        P(None, "dp"),
        P("segment", None, "mp"),
        P("segment", "mp", None),
        P(None, ("segment", "mp")),
    )
    return jax.shard_map(
        on_device,
        mesh=mesh,
        in_specs=placed,
        out_specs=(
            P("dp"),
            P("segment", "dp", "mp"),
            P("segment", "mp", "dp"),
            P("dp", ("segment", "mp")),
        ),
        check_vma=False,
    )
```

profile of v0, /device:TPU:1, one launch (start us, length us, event | category | flops | bytes accessed | tf_op | source)
XLA Modules:
  0.0 2379.7 jit_solution(6565013018614124377)
XLA Ops:
  11.3 113.5 %all-reduce.18.cloned.1.call-done = f32[128,1024]{1,0:T(8,128)} async-done(((f32[128,1024]{1,0:T(8,128)}), f32[128,1024]{1,0:T(8,128)}) %all-reduce.18.cloned.1.call-update) | async-done | bytes 524304 | tf_op jit(solution)/shard_map/psum | solution.py:56
  137.0 111.0 %all-reduce.20.cloned.1.call-done = f32[128,1024]{1,0:T(8,128)} async-done(((f32[128,1024]{1,0:T(8,128)}), f32[128,1024]{1,0:T(8,128)}) %all-reduce.20.cloned.1.call-update) | async-done | bytes 524304 | tf_op jit(solution)/shard_map/psum | solution.py:56
  253.2 5.2 collective-permute-done.1
  261.9 110.8 %all-reduce.22.cloned.1.call-done = f32[128,1024]{1,0:T(8,128)} async-done(((f32[128,1024]{1,0:T(8,128)}), f32[128,1024]{1,0:T(8,128)}) %all-reduce.22.cloned.1.call-update) | async-done | bytes 524304 | tf_op jit(solution)/shard_map/psum | solution.py:56
  377.8 5.2 collective-permute-done.2
  386.5 110.8 %all-reduce.24.cloned.1.call-done = f32[128,1024]{1,0:T(8,128)} async-done(((f32[128,1024]{1,0:T(8,128)}), f32[128,1024]{1,0:T(8,128)}) %all-reduce.24.cloned.1.call-update) | async-done | bytes 524304 | tf_op jit(solution)/shard_map/psum | solution.py:56
  502.4 5.2 collective-permute-done.3
  511.1 110.8 %all-reduce.26.cloned.1.call-done = f32[128,1024]{1,0:T(8,128)} async-done(((f32[128,1024]{1,0:T(8,128)}), f32[128,1024]{1,0:T(8,128)}) %all-reduce.26.cloned.1.call-update) | async-done | bytes 524304 | tf_op jit(solution)/shard_map/psum | solution.py:56
  627.0 5.2 collective-permute-done.4
  635.7 110.8 %all-reduce.28.cloned.1.call-done = f32[128,1024]{1,0:T(8,128)} async-done(((f32[128,1024]{1,0:T(8,128)}), f32[128,1024]{1,0:T(8,128)}) %all-reduce.28.cloned.1.call-update) | async-done | bytes 524304 | tf_op jit(solution)/shard_map/psum | solution.py:56
  760.3 110.8 %all-reduce.30.cloned.1.call-done = f32[128,1024]{1,0:T(8,128)} async-done(((f32[128,1024]{1,0:T(8,128)}), f32[128,1024]{1,0:T(8,128)}) %all-reduce.30.cloned.1.call-update) | async-done | bytes 524304 | tf_op jit(solution)/shard_map/psum | solution.py:56
  876.2 49.1 %all-reduce.32.cloned.1.call-done = bf16[4,128,1024]{2,1,0:T(8,128)(2,1)} async-done(((bf16[4,128,1024]{2,1,0:T(8,128)(2,1)}), bf16[4,128,1024]{2,1,0:T(8,128)(2,1)}) %all-reduce.32.cloned.1.call-update) | async-done | bytes 1048592 | tf_op jit(solution)/shard_map/psum | solution.py:15
  929.3 125.5 %pmax.7 = f32[4,128]{1,0:T(4,128)S(1)} all-reduce(f32[4,128]{1,0:T(4,128)S(1)} %get-tuple-element.40), channel_id=1, replica_groups=mesh['segment'=4,'mp'=16,'dp'=4] {'segment','mp'}, use_global_device_ids=true, to_apply=%region_17.18 | all-reduce | flops 512 | bytes 4096 | tf_op jit(solution)/shard_map/pmax | solution.py:107
  1057.1 127.1 %psum.120 = f32[4,128]{1,0:T(4,128)S(1)} all-reduce(f32[4,128]{1,0:T(4,128)S(1)} %get-tuple-element.12), channel_id=1, replica_groups=mesh['segment'=4,'mp'=16,'dp'=4] {'segment','mp'}, use_global_device_ids=true, to_apply=%region_19.20 | all-reduce | flops 512 | bytes 4096 | tf_op jit(solution)/shard_map/psum | solution.py:108
  1189.2 265.5 %all-reduce.45 = (f32[4,128]{1,0:T(4,128)}, bf16[4,128,1024]{1,0,2:T(4,128)(2,1)}) all-reduce(f32[4,128]{1,0:T(4,128)S(1)} %get-tuple-element.13, f32[4,128,1024]{1,0,2:T(4,128)} %copy.13), channel_id=1, replica_groups=mesh['segment'=4,'mp'=16,'dp'=4] {'segment','mp'}, use_global_device_ids=true, to_apply=%region_23.24 | all-reduce | flops 524800 | bytes 3149824 | tf_op jit(solution)/shard_map/psum | solution.py:108
  1456.9 75.1 %all-gather.2.cloned.1.call-done = bf16[4,128,1024]{1,0,2:T(4,128)(2,1)} async-done(((bf16[4,128,16]{1,0,2:T(4,128)(2,1)}), bf16[4,128,1024]{1,0,2:T(4,128)(2,1)}) %all-gather.2.cloned.1.call-update) | async-done | bytes 1048592 | tf_op jit(solution)/shard_map/all_gather | solution.py:124
  1540.1 106.9 %all-reduce.34.cloned.1.call-done = f32[128,1024]{1,0:T(8,128)} async-done(((f32[128,1024]{1,0:T(8,128)}), f32[128,1024]{1,0:T(8,128)}) %all-reduce.34.cloned.1.call-update) | async-done | bytes 524304 | tf_op jit(solution)/shard_map/psum | solution.py:56
  1651.1 7.3 collective-permute-done.6
  1661.0 109.8 %all-reduce.36.cloned.1.call-done = f32[128,1024]{1,0:T(8,128)} async-done(((f32[128,1024]{1,0:T(8,128)}), f32[128,1024]{1,0:T(8,128)}) %all-reduce.36.cloned.1.call-update) | async-done | bytes 524304 | tf_op jit(solution)/shard_map/psum | solution.py:56
  1775.8 6.7 collective-permute-done.7
  1786.7 109.8 %all-reduce.38.cloned.1.call-done = f32[128,1024]{1,0:T(8,128)} async-done(((f32[128,1024]{1,0:T(8,128)}), f32[128,1024]{1,0:T(8,128)}) %all-reduce.38.cloned.1.call-update) | async-done | bytes 524304 | tf_op jit(solution)/shard_map/psum | solution.py:56
  1901.5 6.7 collective-permute-done.8
  1912.4 109.8 %all-reduce.40.cloned.1.call-done = f32[128,1024]{1,0:T(8,128)} async-done(((f32[128,1024]{1,0:T(8,128)}), f32[128,1024]{1,0:T(8,128)}) %all-reduce.40.cloned.1.call-update) | async-done | bytes 524304 | tf_op jit(solution)/shard_map/psum | solution.py:56
  2027.3 6.7 collective-permute-done.9
  2038.2 109.8 %all-reduce.42.cloned.1.call-done = f32[128,1024]{1,0:T(8,128)} async-done(((f32[128,1024]{1,0:T(8,128)}), f32[128,1024]{1,0:T(8,128)}) %all-reduce.42.cloned.1.call-update) | async-done | bytes 524304 | tf_op jit(solution)/shard_map/psum | solution.py:56
  2153.0 6.7 collective-permute-done.10
  2178.9 94.8 %all-reduce.44.cloned.1.call-done = f32[128,1024]{1,0:T(8,128)} async-done(((f32[128,1024]{1,0:T(8,128)}), f32[128,1024]{1,0:T(8,128)}) %all-reduce.44.cloned.1.call-update) | async-done | bytes 524304 | tf_op jit(solution)/shard_map/psum | solution.py:56
  2278.2 7.3 collective-permute-done.11
  2286.2 6.7 multiply_add_fusion
  2305.0 7.7 multiply_add_fusion.1
  2314.6 21.9 reduce-scatter.6.cloned.1.call-done
  2336.6 35.2 %reduce-scatter.4.cloned.1.call-done = f32[256,512]{1,0:T(8,128)} async-done(((f32[1024,512]{1,0:T(8,128)}), f32[256,512]{1,0:T(8,128)}) %reduce-scatter.4.cloned.1.call-update) | async-done | bytes 524304 | tf_op jit(solution)/shard_map/reduce_scatter | solution.py:154
  (293 shorter events, 166.7 us)
Async XLA Ops:
  7.2 117.6 %all-reduce.18.cloned.1.call-start = ((), (), s32[]{:S(2)}) async-start(), calls=%async_computation.3 | async-start | bytes 1048576 | tf_op jit(solution)/shard_map/psum | solution.py:56
  11.2 236.8 %all-reduce.20.cloned.1.call-start = ((), (), s32[]{:S(2)}) async-start(), calls=%async_computation.4 | async-start | bytes 1048576 | tf_op jit(solution)/shard_map/psum | solution.py:56
  126.2 8.0 collective-permute-start
  137.0 235.7 %all-reduce.22.cloned.1.call-start = ((), (), s32[]{:S(2)}) async-start(), calls=%async_computation.5 | async-start | bytes 1048576 | tf_op jit(solution)/shard_map/psum | solution.py:56
  250.1 8.3 collective-permute-start.1
  261.8 235.4 %all-reduce.24.cloned.1.call-start = ((), (), s32[]{:S(2)}) async-start(), calls=%async_computation.6 | async-start | bytes 1048576 | tf_op jit(solution)/shard_map/psum | solution.py:56
  374.7 8.3 collective-permute-start.2
  386.4 235.4 %all-reduce.26.cloned.1.call-start = ((), (), s32[]{:S(2)}) async-start(), calls=%async_computation.7 | async-start | bytes 1048576 | tf_op jit(solution)/shard_map/psum | solution.py:56
  499.3 8.3 collective-permute-start.3
  511.0 235.4 %all-reduce.28.cloned.1.call-start = ((), (), s32[]{:S(2)}) async-start(), calls=%async_computation.8 | async-start | bytes 1048576 | tf_op jit(solution)/shard_map/psum | solution.py:56
  623.9 8.3 collective-permute-start.4
  635.7 235.4 %all-reduce.30.cloned.1.call-start = ((), (), s32[]{:S(2)}) async-start(), calls=%async_computation.9 | async-start | bytes 1048576 | tf_op jit(solution)/shard_map/psum | solution.py:56
  748.5 8.3 collective-permute-start.5
  760.3 165.0 %all-reduce.32.cloned.1.call-start = ((), (), s32[]{:S(2)}) async-start(), calls=%async_computation.10 | async-start | bytes 2097152 | tf_op jit(solution)/shard_map/psum | solution.py:15
  874.2 180.6 %copy-start.59 = (s32[4,512]{1,0:T(4,128)S(1)}, s32[4,512]{1,0:T(4,128)}, u32[]{:S(2)}) copy-start(s32[4,512]{1,0:T(4,128)} %param.8) | copy-start | bytes 24580
  874.2 657.7 %all-gather.2.cloned.1.call-start = ((), (), s32[]{:S(2)}) async-start(), calls=%async_computation.11 | async-start | bytes 1064960 | tf_op jit(solution)/shard_map/all_gather | solution.py:124
  1456.1 190.9 %all-reduce.34.cloned.1.call-start = ((), (), s32[]{:S(2)}) async-start(), calls=%async_computation.12 | async-start | bytes 1048576 | tf_op jit(solution)/shard_map/psum | solution.py:56
  1456.5 192.7 %copy-start.55 = (f32[128]{0:T(128)}, f32[128]{0:T(128)S(1)}, u32[]{:S(2)}) copy-start(f32[128]{0:T(128)S(1)} %add_rsqrt_fusion.7) | copy-start | bytes 1540
  1540.0 230.8 %all-reduce.36.cloned.1.call-start = ((), (), s32[]{:S(2)}) async-start(), calls=%async_computation.13 | async-start | bytes 1048576 | tf_op jit(solution)/shard_map/psum | solution.py:56
  1649.4 9.0 collective-permute-start.6
  1661.0 235.5 %all-reduce.38.cloned.1.call-start = ((), (), s32[]{:S(2)}) async-start(), calls=%async_computation.14 | async-start | bytes 1048576 | tf_op jit(solution)/shard_map/psum | solution.py:56
  1773.4 9.0 collective-permute-start.7
  1786.6 235.6 %all-reduce.40.cloned.1.call-start = ((), (), s32[]{:S(2)}) async-start(), calls=%async_computation.15 | async-start | bytes 1048576 | tf_op jit(solution)/shard_map/psum | solution.py:56
  1899.1 9.0 collective-permute-start.8
  1912.4 235.6 %all-reduce.42.cloned.1.call-start = ((), (), s32[]{:S(2)}) async-start(), calls=%async_computation.16 | async-start | bytes 1048576 | tf_op jit(solution)/shard_map/psum | solution.py:56
  2024.9 9.0 collective-permute-start.9
  2038.1 235.6 %all-reduce.44.cloned.1.call-start = ((), (), s32[]{:S(2)}) async-start(), calls=%async_computation.17 | async-start | bytes 1048576 | tf_op jit(solution)/shard_map/psum | solution.py:56
  2150.7 9.0 collective-permute-start.10
  2163.9 150.7 %reduce-scatter.8.cloned.1.call-start = ((), (), s32[]{:S(2)}) async-start(), calls=%async_computation.20 | async-start | bytes 819200 | tf_op jit(solution)/shard_map/reduce_scatter | solution.py:156
  2166.6 169.9 %reduce-scatter.6.cloned.1.call-start = ((), (), s32[]{:S(2)}) async-start(), calls=%async_computation.19 | async-start | bytes 2621440 | tf_op jit(solution)/shard_map/reduce_scatter | solution.py:155
  2276.5 9.0 collective-permute-start.11
  2292.9 78.8 %reduce-scatter.4.cloned.1.call-start = ((), (), s32[]{:S(2)}) async-start(), calls=%async_computation.18 | async-start | bytes 2621440 | tf_op jit(solution)/shard_map/reduce_scatter | solution.py:154
  (59 other events, 808.3 us)
Sparse Core Ops, SparseCore 0:
  11.4 113.3 all-reduce.17
  137.1 110.8 all-reduce.19
  261.9 110.6 all-reduce.21
  386.5 110.6 all-reduce.23
  511.2 110.6 all-reduce.25
  635.8 110.6 all-reduce.27
  760.4 110.6 all-reduce.29
  874.3 50.9 all-reduce.31
  1456.2 75.6 all-gather.1
  1540.1 106.8 all-reduce.33
  1661.1 109.7 all-reduce.35
  1786.8 109.7 all-reduce.37
  1912.5 109.7 all-reduce.39
  2038.3 109.7 all-reduce.41
  2164.0 109.6 all-reduce.43
  2276.7 23.4 reduce-scatter.7
  2303.2 33.2 reduce-scatter.5
  2339.7 31.9 reduce-scatter.3
where the time goes:
time: 2380 us
  waiting for transfers between devices  1670 us (70%)
  blocking collectives  518 us (22%)
  matrix products  70.9 us (3%)
  other arithmetic  53.3 us (2%)
  starting transfers between devices  28.3 us (1%)
    psum x13, waiting for transfers between devices, reduce_rows(): summed = lax.psum(partial_value, 'mp')  1420 us
    psum x2, blocking collectives, on_device(): lax.psum((jnp.sum(jnp.exp(logits - peak[..., None]), axis=-1), target_loc...  393 us
    pmax x1, blocking collectives, on_device(): peak = lax.pmax(local_peak, ('segment', 'mp'))  125 us
    all_gather x1, waiting for transfers between devices, on_device(): dnorm = lax.all_gather(norm_share, ('segment', 'mp'), axis=2, tiled=True)  75.1 us
    ppermute x12, waiting for transfers between devices, shifted(): return lax.ppermute(block, axis, route)  70.4 us
    psum x1, waiting for transfers between devices, broadcast(): return lax.psum(jnp.where(mine, x, jnp.zeros_like(x)), axis)  49.1 us
  transfers between devices with their start and end apart: 30, of which 29 were waited for; matrix products, arithmetic and copies ran while one was open for 2% of the time, Pallas kernels for 0%

commit v1 on v0

--- a/solution.py
+++ b/solution.py
@@ -106,7 +106,8 @@
     target_local = jnp.sum(counts * logits, axis=-1)
     peak = lax.pmax(local_peak, ("segment", "mp"))
     total, target_sum = lax.psum(
-        (jnp.sum(jnp.exp(logits - peak[..., None]), axis=-1), target_local), ("segment", "mp")
+        lax.psum((jnp.sum(jnp.exp(logits - peak[..., None]), axis=-1), target_local), "segment"),
+        "mp",
     )
     lse = peak + jnp.log(total)
     denom = float(micro_count * unit_count * lax.axis_size("dp"))

time: 2380 us -> 2290 us (0.962)
  blocking collectives: 518 us -> 423 us
    psum x2 -> x1, blocking collectives: 393 us -> 5.97 us  [on_device(): lax.psum((jnp.sum(jnp.exp(logits - peak[..., None]), axis=-1), target_loc...]
    unnamed x0 -> x1, blocking collectives: none -> 263 us
    psum x0 -> x1, blocking collectives: none -> 28.3 us  [on_device(): lax.psum(lax.psum((jnp.sum(jnp.exp(logits - peak[..., None]), axis=-1), t...]
where the time goes in v1:
time: 2290 us; the launch traced here: 2280 us
  waiting for transfers between devices  1670 us (73%)
  blocking collectives  423 us (18%)
  matrix products  70.2 us (3%)
  other arithmetic  53.2 us (2%)
  starting transfers between devices  28.3 us (1%)
    psum x13, waiting for transfers between devices, reduce_rows(): summed = lax.psum(partial_value, 'mp')  1420 us
    unnamed x1, blocking collectives  263 us
    pmax x1, blocking collectives, on_device(): peak = lax.pmax(local_peak, ('segment', 'mp'))  125 us
    all_gather x1, waiting for transfers between devices, on_device(): dnorm = lax.all_gather(norm_share, ('segment', 'mp'), axis=2, tiled=True)  75 us
    ppermute x12, waiting for transfers between devices, shifted(): return lax.ppermute(block, axis, route)  70.6 us
    psum x1, waiting for transfers between devices, broadcast(): return lax.psum(jnp.where(mine, x, jnp.zeros_like(x)), axis)  49.1 us
  transfers between devices with their start and end apart: 30, of which 29 were waited for; matrix products, arithmetic and copies ran while one was open for 2% of the time, Pallas kernels for 0%

profile of v1, /device:TPU:1, one launch (start us, length us, event | category | flops | bytes accessed | tf_op | source)
XLA Modules:
  0.0 2285.0 jit_solution(3971366425841515006)
XLA Ops:
  11.3 113.5 %all-reduce.19.cloned.1.call-done = f32[128,1024]{1,0:T(8,128)} async-done(((f32[128,1024]{1,0:T(8,128)}), f32[128,1024]{1,0:T(8,128)}) %all-reduce.19.cloned.1.call-update) | async-done | bytes 524304 | tf_op jit(solution)/shard_map/psum | solution.py:56
  137.0 111.0 %all-reduce.21.cloned.1.call-done = f32[128,1024]{1,0:T(8,128)} async-done(((f32[128,1024]{1,0:T(8,128)}), f32[128,1024]{1,0:T(8,128)}) %all-reduce.21.cloned.1.call-update) | async-done | bytes 524304 | tf_op jit(solution)/shard_map/psum | solution.py:56
  253.2 5.2 collective-permute-done.1
  261.9 110.8 %all-reduce.23.cloned.1.call-done = f32[128,1024]{1,0:T(8,128)} async-done(((f32[128,1024]{1,0:T(8,128)}), f32[128,1024]{1,0:T(8,128)}) %all-reduce.23.cloned.1.call-update) | async-done | bytes 524304 | tf_op jit(solution)/shard_map/psum | solution.py:56
  377.8 5.2 collective-permute-done.2
  386.5 110.8 %all-reduce.25.cloned.1.call-done = f32[128,1024]{1,0:T(8,128)} async-done(((f32[128,1024]{1,0:T(8,128)}), f32[128,1024]{1,0:T(8,128)}) %all-reduce.25.cloned.1.call-update) | async-done | bytes 524304 | tf_op jit(solution)/shard_map/psum | solution.py:56
  511.1 110.8 %all-reduce.27.cloned.1.call-done = f32[128,1024]{1,0:T(8,128)} async-done(((f32[128,1024]{1,0:T(8,128)}), f32[128,1024]{1,0:T(8,128)}) %all-reduce.27.cloned.1.call-update) | async-done | bytes 524304 | tf_op jit(solution)/shard_map/psum | solution.py:56
  635.7 110.8 %all-reduce.29.cloned.1.call-done = f32[128,1024]{1,0:T(8,128)} async-done(((f32[128,1024]{1,0:T(8,128)}), f32[128,1024]{1,0:T(8,128)}) %all-reduce.29.cloned.1.call-update) | async-done | bytes 524304 | tf_op jit(solution)/shard_map/psum | solution.py:56
  751.7 5.2 collective-permute-done.5
  760.4 110.8 %all-reduce.31.cloned.1.call-done = f32[128,1024]{1,0:T(8,128)} async-done(((f32[128,1024]{1,0:T(8,128)}), f32[128,1024]{1,0:T(8,128)}) %all-reduce.31.cloned.1.call-update) | async-done | bytes 524304 | tf_op jit(solution)/shard_map/psum | solution.py:56
  876.2 49.1 %all-reduce.33.cloned.1.call-done = bf16[4,128,1024]{2,1,0:T(8,128)(2,1)} async-done(((bf16[4,128,1024]{2,1,0:T(8,128)(2,1)}), bf16[4,128,1024]{2,1,0:T(8,128)(2,1)}) %all-reduce.33.cloned.1.call-update) | async-done | bytes 1048592 | tf_op jit(solution)/shard_map/psum | solution.py:15
  929.4 125.5 %pmax.7 = f32[4,128]{1,0:T(4,128)S(1)} all-reduce(f32[4,128]{1,0:T(4,128)S(1)} %get-tuple-element.44), channel_id=1, replica_groups=mesh['segment'=4,'mp'=16,'dp'=4] {'segment','mp'}, use_global_device_ids=true, to_apply=%region_17.18 | all-reduce | flops 512 | bytes 4096 | tf_op jit(solution)/shard_map/pmax | solution.py:107
  1057.1 6.0 all-reduce.2
  1063.1 28.3 %all-reduce.1 = (f32[4,128]{1,0:T(4,128)S(1)}, f32[4,128]{1,0:T(4,128)S(1)}) all-reduce(f32[4,128]{1,0:T(4,128)S(1)} %get-tuple-element.16, f32[4,128]{1,0:T(4,128)S(1)} %get-tuple-element.17), channel_id=1, replica_groups=mesh['segment'=4,'mp'=16,'dp'=4] {'mp'}, use_global_device_ids=true, to_apply=%region_25.26 | all-reduce | flops 1024 | bytes 8192 | tf_op jit(solution)/shard_map/psum | solution.py:108
  1097.1 263.5 %all-reduce.46 = bf16[4,128,1024]{1,0,2:T(4,128)(2,1)} all-reduce(f32[4,128,1024]{1,0,2:T(4,128)} %copy.13), channel_id=2, replica_groups=mesh['segment'=4,'mp'=16,'dp'=4] {'segment','mp'}, use_global_device_ids=true, to_apply=%region_28.29.clone | all-reduce | flops 524288 | bytes 3145728
  1362.7 75.0 %all-gather.2.cloned.1.call-done = bf16[4,128,1024]{1,0,2:T(4,128)(2,1)} async-done(((bf16[4,128,16]{1,0,2:T(4,128)(2,1)}), bf16[4,128,1024]{1,0,2:T(4,128)(2,1)}) %all-gather.2.cloned.1.call-update) | async-done | bytes 1048592 | tf_op jit(solution)/shard_map/all_gather | solution.py:125
  1445.8 106.8 %all-reduce.35.cloned.1.call-done = f32[128,1024]{1,0:T(8,128)} async-done(((f32[128,1024]{1,0:T(8,128)}), f32[128,1024]{1,0:T(8,128)}) %all-reduce.35.cloned.1.call-update) | async-done | bytes 524304 | tf_op jit(solution)/shard_map/psum | solution.py:56
  1556.6 7.3 collective-permute-done.6
  1566.6 109.8 %all-reduce.37.cloned.1.call-done = f32[128,1024]{1,0:T(8,128)} async-done(((f32[128,1024]{1,0:T(8,128)}), f32[128,1024]{1,0:T(8,128)}) %all-reduce.37.cloned.1.call-update) | async-done | bytes 524304 | tf_op jit(solution)/shard_map/psum | solution.py:56
  1681.3 6.7 collective-permute-done.7
  1692.2 109.6 %all-reduce.39.cloned.1.call-done = f32[128,1024]{1,0:T(8,128)} async-done(((f32[128,1024]{1,0:T(8,128)}), f32[128,1024]{1,0:T(8,128)}) %all-reduce.39.cloned.1.call-update) | async-done | bytes 524304 | tf_op jit(solution)/shard_map/psum | solution.py:56
  1806.8 6.7 collective-permute-done.8
  1817.7 109.8 %all-reduce.41.cloned.1.call-done = f32[128,1024]{1,0:T(8,128)} async-done(((f32[128,1024]{1,0:T(8,128)}), f32[128,1024]{1,0:T(8,128)}) %all-reduce.41.cloned.1.call-update) | async-done | bytes 524304 | tf_op jit(solution)/shard_map/psum | solution.py:56
  1932.5 6.8 collective-permute-done.9
  1943.5 109.8 %all-reduce.43.cloned.1.call-done = f32[128,1024]{1,0:T(8,128)} async-done(((f32[128,1024]{1,0:T(8,128)}), f32[128,1024]{1,0:T(8,128)}) %all-reduce.43.cloned.1.call-update) | async-done | bytes 524304 | tf_op jit(solution)/shard_map/psum | solution.py:56
  2058.3 6.7 collective-permute-done.10
  2084.2 94.8 %all-reduce.45.cloned.1.call-done = f32[128,1024]{1,0:T(8,128)} async-done(((f32[128,1024]{1,0:T(8,128)}), f32[128,1024]{1,0:T(8,128)}) %all-reduce.45.cloned.1.call-update) | async-done | bytes 524304 | tf_op jit(solution)/shard_map/psum | solution.py:56
  2183.4 7.3 collective-permute-done.11
  2191.5 6.7 multiply_add_fusion
  2210.1 7.7 multiply_add_fusion.1
  2218.5 23.4 %reduce-scatter.6.cloned.1.call-done = f32[512,256]{1,0:T(8,128)} async-done(((f32[512,1024]{1,0:T(8,128)}), f32[512,256]{1,0:T(8,128)}) %reduce-scatter.6.cloned.1.call-update) | async-done | bytes 524304 | tf_op jit(solution)/shard_map/reduce_scatter | solution.py:156
  2241.8 35.2 %reduce-scatter.4.cloned.1.call-done = f32[256,512]{1,0:T(8,128)} async-done(((f32[1024,512]{1,0:T(8,128)}), f32[256,512]{1,0:T(8,128)}) %reduce-scatter.4.cloned.1.call-update) | async-done | bytes 524304 | tf_op jit(solution)/shard_map/reduce_scatter | solution.py:155
  (285 shorter events, 170.9 us)
Async XLA Ops:
  7.2 117.6 %all-reduce.19.cloned.1.call-start = ((), (), s32[]{:S(2)}) async-start(), calls=%async_computation.3 | async-start | bytes 1048576 | tf_op jit(solution)/shard_map/psum | solution.py:56
  11.2 236.8 %all-reduce.21.cloned.1.call-start = ((), (), s32[]{:S(2)}) async-start(), calls=%async_computation.4 | async-start | bytes 1048576 | tf_op jit(solution)/shard_map/psum | solution.py:56
  126.2 8.0 collective-permute-start
  137.0 235.7 %all-reduce.23.cloned.1.call-start = ((), (), s32[]{:S(2)}) async-start(), calls=%async_computation.5 | async-start | bytes 1048576 | tf_op jit(solution)/shard_map/psum | solution.py:56
  250.1 8.3 collective-permute-start.1
  261.8 235.4 %all-reduce.25.cloned.1.call-start = ((), (), s32[]{:S(2)}) async-start(), calls=%async_computation.6 | async-start | bytes 1048576 | tf_op jit(solution)/shard_map/psum | solution.py:56
  374.7 8.3 collective-permute-start.2
  386.4 235.4 %all-reduce.27.cloned.1.call-start = ((), (), s32[]{:S(2)}) async-start(), calls=%async_computation.7 | async-start | bytes 1048576 | tf_op jit(solution)/shard_map/psum | solution.py:56
  499.3 8.3 collective-permute-start.3
  511.1 235.5 %all-reduce.29.cloned.1.call-start = ((), (), s32[]{:S(2)}) async-start(), calls=%async_computation.8 | async-start | bytes 1048576 | tf_op jit(solution)/shard_map/psum | solution.py:56
  623.9 8.3 collective-permute-start.4
  635.7 235.5 %all-reduce.31.cloned.1.call-start = ((), (), s32[]{:S(2)}) async-start(), calls=%async_computation.9 | async-start | bytes 1048576 | tf_op jit(solution)/shard_map/psum | solution.py:56
  748.6 8.3 collective-permute-start.5
  760.3 165.0 %all-reduce.33.cloned.1.call-start = ((), (), s32[]{:S(2)}) async-start(), calls=%async_computation.10 | async-start | bytes 2097152 | tf_op jit(solution)/shard_map/psum | solution.py:15
  874.2 180.6 %copy-start.55 = (s32[4,512]{1,0:T(4,128)S(1)}, s32[4,512]{1,0:T(4,128)}, u32[]{:S(2)}) copy-start(s32[4,512]{1,0:T(4,128)} %param.8) | copy-start | bytes 24580
  874.2 563.5 %all-gather.2.cloned.1.call-start = ((), (), s32[]{:S(2)}) async-start(), calls=%async_computation.11 | async-start | bytes 1064960 | tf_op jit(solution)/shard_map/all_gather | solution.py:125
  1361.9 190.6 %all-reduce.35.cloned.1.call-start = ((), (), s32[]{:S(2)}) async-start(), calls=%async_computation.12 | async-start | bytes 1048576 | tf_op jit(solution)/shard_map/psum | solution.py:56
  1362.3 192.4 %copy-start.51 = (f32[128]{0:T(128)}, f32[128]{0:T(128)S(1)}, u32[]{:S(2)}) copy-start(f32[128]{0:T(128)S(1)} %add_rsqrt_fusion.7) | copy-start | bytes 1540
  1445.7 230.7 %all-reduce.37.cloned.1.call-start = ((), (), s32[]{:S(2)}) async-start(), calls=%async_computation.13 | async-start | bytes 1048576 | tf_op jit(solution)/shard_map/psum | solution.py:56
  1555.0 9.0 collective-permute-start.6
  1566.5 235.3 %all-reduce.39.cloned.1.call-start = ((), (), s32[]{:S(2)}) async-start(), calls=%async_computation.14 | async-start | bytes 1048576 | tf_op jit(solution)/shard_map/psum | solution.py:56
  1679.0 9.0 collective-permute-start.7
  1692.2 235.4 %all-reduce.41.cloned.1.call-start = ((), (), s32[]{:S(2)}) async-start(), calls=%async_computation.15 | async-start | bytes 1048576 | tf_op jit(solution)/shard_map/psum | solution.py:56
  1804.5 9.0 collective-permute-start.8
  1817.7 235.6 %all-reduce.43.cloned.1.call-start = ((), (), s32[]{:S(2)}) async-start(), calls=%async_computation.16 | async-start | bytes 1048576 | tf_op jit(solution)/shard_map/psum | solution.py:56
  1930.2 9.0 collective-permute-start.9
  1943.4 235.6 %all-reduce.45.cloned.1.call-start = ((), (), s32[]{:S(2)}) async-start(), calls=%async_computation.17 | async-start | bytes 1048576 | tf_op jit(solution)/shard_map/psum | solution.py:56
  2055.9 9.0 collective-permute-start.10
  2069.2 149.3 %reduce-scatter.8.cloned.1.call-start = ((), (), s32[]{:S(2)}) async-start(), calls=%async_computation.20 | async-start | bytes 819200 | tf_op jit(solution)/shard_map/reduce_scatter | solution.py:157
  2071.9 170.0 %reduce-scatter.6.cloned.1.call-start = ((), (), s32[]{:S(2)}) async-start(), calls=%async_computation.19 | async-start | bytes 2621440 | tf_op jit(solution)/shard_map/reduce_scatter | solution.py:156
  2181.8 9.0 collective-permute-start.11
  2198.2 78.8 %reduce-scatter.4.cloned.1.call-start = ((), (), s32[]{:S(2)}) async-start(), calls=%async_computation.18 | async-start | bytes 2621440 | tf_op jit(solution)/shard_map/reduce_scatter | solution.py:155
  (55 other events, 548.5 us)
Sparse Core Ops, SparseCore 0:
  11.4 113.3 all-reduce.18
  137.1 110.8 all-reduce.20
  261.9 110.6 all-reduce.22
  386.6 110.6 all-reduce.24
  511.2 110.6 all-reduce.26
  635.8 110.6 all-reduce.28
  760.4 110.6 all-reduce.30
  874.4 50.9 all-reduce.32
  1362.0 75.6 all-gather.1
  1445.9 106.6 all-reduce.34
  1566.6 109.7 all-reduce.36
  1692.3 109.5 all-reduce.38
  1817.8 109.7 all-reduce.40
  1943.5 109.7 all-reduce.42
  2069.3 109.7 all-reduce.44
  2182.0 23.4 reduce-scatter.7
  2208.5 33.2 reduce-scatter.5
  2245.0 31.9 reduce-scatter.3
